TPU v7x, 512 devices: a whole 4x4x16 slice. The times are simulated.
512 devices in a mesh: sample: 32 (over x, y, core), cls: 16 (over z).
Axes of the slice: x: 4, y: 4, z: 16, core: 2. Of those that a mesh axis runs over, the one named last changes fastest.
Arguments:
- features: bfloat16 [16384, 2048], P('sample', 'cls'), may hold values from -1.5 to 1.5
- head: bfloat16 [2048, 8192], P('sample', 'cls'), may hold values from -1.5859375 to 1.5859375
- class_cap: bfloat16 [8192], P('cls'), may hold values from 0.5 to 4
Outputs:
- targets: bfloat16 [16384, 8192], P('sample', 'cls')
- grad_features: bfloat16 [16384, 2048], P('sample', 'cls')
- grad_head: bfloat16 [2048, 8192], P('sample', 'cls')
All inputs are finite; a program needn't handle non-finite values.
Results may differ from a plain program's by a relative error of at most 0.02.
Values may be sent and summed in bfloat16 or wider, within the bound.
A program may use at most 64 MiB of HBM per device.

v0:
```python
import jax
import jax.numpy as jnp
from jax import lax
from jax.sharding import PartitionSpec as P

ITERS = 3
softcap = 15.0
sharpen = 2.0


def row_total(values):
    return lax.psum(jnp.sum(values, axis=1), "cls")


def per_device(features, head, class_cap):
    local_rows = features.shape[0]
    class_local = head.shape[1]
    sample_count = lax.axis_size("sample")
    class_groups = lax.axis_size("cls")
    ratio = local_rows * sample_count / (class_local * class_groups)
    whole = lax.all_gather(features, "cls", axis=1, tiled=True)
    head_full = lax.all_gather(head, "sample", axis=0, tiled=True)
    logits = jnp.dot(whole, head_full, preferred_element_type=jnp.float32)
    capped = softcap * jnp.tanh(logits / softcap)
    student = jnp.exp(capped)
    transport = jnp.exp(capped * sharpen)
    student_mass, plan_mass = lax.psum(
        (jnp.sum(student, axis=1), jnp.sum(transport, axis=1)), "cls"
    )
    student = student / student_mass[:, None]
    ceiling = class_cap.astype(jnp.float32) * ratio
    for iteration in range(ITERS):
        if iteration > 0:
            plan_mass = row_total(transport)
        transport = transport / plan_mass[:, None]
        column_mass = lax.psum(jnp.sum(transport, axis=0), "sample")
        transport = transport * jnp.minimum(1.0, ceiling / column_mass)
    targets = (transport / row_total(transport)[:, None]).astype(jnp.bfloat16)
    tanh_slope = 1.0 - (capped / softcap) ** 2
    grad_logits = ((student - targets.astype(jnp.float32)) * tanh_slope).astype(jnp.bfloat16)
    grad_head = lax.psum_scatter(
        lax.dot_general(
            whole, grad_logits, (((0,), (0,)), ((), ())), preferred_element_type=jnp.float32
        ).astype(jnp.bfloat16),
        "sample",
        scatter_dimension=0,
        tiled=True,
    )
    share = lax.psum_scatter(
        lax.dot_general(
            head_full, grad_logits, (((1,), (1,)), ((), ())), preferred_element_type=jnp.float32
        ).astype(jnp.bfloat16),
        "cls",
        scatter_dimension=0,
        tiled=True,
    ).astype(jnp.float32)
    grad_features = jnp.transpose(share).astype(jnp.bfloat16)
    return (targets, grad_features, grad_head)


def solution(mesh):
    return jax.shard_map(
        per_device,
        mesh=mesh,
        in_specs=(P("sample", "cls"), P("sample", "cls"), P("cls")),
        out_specs=(P("sample", "cls"), P("sample", "cls"), P("sample", "cls")),
        check_vma=False,
    )
```

profile of v0, /device:TPU:2, one launch (start us, length us, event | category | flops | bytes accessed | tf_op | source)
XLA Modules:
  0.0 643.5 jit_solution(15477664846677126857)
XLA Ops:
  7.2 0.7 all-gather.3.cloned.1.call-update
  7.9 0.7 all-gather.5.cloned.1.call-update
  8.7 85.0 %all-gather.3.cloned.1.call-done = bf16[512,2048]{1,0:T(8,128)(2,1)} async-done(((bf16[512,128]{1,0:T(8,128)(2,1)}), bf16[512,2048]{1,0:T(8,128)(2,1)}) %all-gather.3.cloned.1.call-update) | async-done | bytes 2097168 | tf_op jit(solution)/shard_map/all_gather | solution.py:21
  93.7 57.1 %all-gather.5.cloned.1.call-done = bf16[2048,512]{1,0:T(8,128)(2,1)} async-done(((bf16[64,512]{1,0:T(8,128)(2,1)}), bf16[2048,512]{1,0:T(8,128)(2,1)}) %all-gather.5.cloned.1.call-update) | async-done | bytes 2097168 | tf_op jit(solution)/shard_map/all_gather | solution.py:22
  150.9 3.7 fusion.5
  154.6 31.3 %psum.56 = f32[512]{0:T(512)S(1)} all-reduce(f32[512]{0:T(512)S(1)} %get-tuple-element.17), channel_id=1, replica_groups=mesh['sample'=32,'cls'=16] {'cls'}, use_global_device_ids=true, to_apply=%region_1.0 | all-reduce | flops 512 | bytes 4096 | tf_op jit(solution)/shard_map/psum | solution.py:27
  186.1 53.0 %psum.57 = f32[512]{0:T(512)S(1)} all-reduce(f32[512]{0:T(512)S(1)} %fusion.12), channel_id=1, replica_groups=mesh['sample'=32,'cls'=16] {'sample'}, use_global_device_ids=true, to_apply=%region_3.0 | all-reduce | flops 512 | bytes 4096 | tf_op jit(solution)/shard_map/psum | solution.py:36
  239.1 0.4 fusion.3
  239.5 28.4 %psum.58 = f32[512]{0:T(512)S(1)} all-reduce(f32[512]{0:T(512)S(1)} %get-tuple-element.10), channel_id=1, replica_groups=mesh['sample'=32,'cls'=16] {'cls'}, use_global_device_ids=true, to_apply=%region_5.0 | all-reduce | flops 512 | bytes 4096 | tf_op jit(solution)/shard_map/psum | solution.py:12
  267.8 0.3 fusion.14
  268.2 55.0 %psum.59 = f32[512]{0:T(512)S(1)} all-reduce(f32[512]{0:T(512)S(1)} %get-tuple-element.15), channel_id=1, replica_groups=mesh['sample'=32,'cls'=16] {'sample'}, use_global_device_ids=true, to_apply=%region_7.0 | all-reduce | flops 512 | bytes 4096 | tf_op jit(solution)/shard_map/psum | solution.py:36
  323.4 28.9 %psum.60 = f32[512]{0:T(512)S(1)} all-reduce(f32[512]{0:T(512)S(1)} %multiply_reduce_fusion.1), channel_id=1, replica_groups=mesh['sample'=32,'cls'=16] {'cls'}, use_global_device_ids=true, to_apply=%region_9.0 | all-reduce | flops 512 | bytes 4096 | tf_op jit(solution)/shard_map/psum | solution.py:12
  352.5 62.7 %psum.61 = f32[512]{0:T(512)S(1)} all-reduce(f32[512]{0:T(512)S(1)} %fusion.13), channel_id=1, replica_groups=mesh['sample'=32,'cls'=16] {'sample'}, use_global_device_ids=true, to_apply=%region_11.0 | all-reduce | flops 512 | bytes 4096 | tf_op jit(solution)/shard_map/psum | solution.py:36
  415.4 27.9 %all-reduce = (f32[512]{0:T(512)S(1)}, f32[512]{0:T(512)S(1)}) all-reduce(f32[512]{0:T(512)S(1)} %multiply_reduce_fusion, f32[512]{0:T(512)S(1)} %get-tuple-element.9), channel_id=1, replica_groups=mesh['sample'=32,'cls'=16] {'cls'}, use_global_device_ids=true, to_apply=%region_13.0 | all-reduce | flops 1024 | bytes 8192 | tf_op jit(solution)/shard_map/psum | solution.py:12
  443.3 0.5 multiply_convert_fusion
  443.8 1.1 copy-done.1
  444.9 1.3 fusion
  446.2 2.6 copy.10
  448.8 2.8 fusion.1
  451.7 2.5 copy.12
  454.2 1.0 copy.8
  455.2 77.6 %reduce-scatter.7.cloned.1.call-done = bf16[128,512]{1,0:T(8,128)(2,1)} async-done(((bf16[2048,512]{1,0:T(8,128)(2,1)}), bf16[128,512]{1,0:T(8,128)(2,1)}) %reduce-scatter.7.cloned.1.call-update) | async-done | bytes 131088
  532.9 1.7 copy.11
  534.5 102.4 %reduce-scatter.9.cloned.1.call-done = bf16[64,512]{1,0:T(8,128)(2,1)} async-done(((bf16[2048,512]{1,0:T(8,128)(2,1)}), bf16[64,512]{1,0:T(8,128)(2,1)}) %reduce-scatter.9.cloned.1.call-update) | async-done | bytes 65552
  (16 shorter events, 1.1 us)
Async XLA Ops:
  7.2 86.6 %all-gather.3.cloned.1.call-start = ((), (), s32[]{:S(2)}) async-start(), calls=%async_computation.2 | async-start | bytes 2228224 | tf_op jit(solution)/shard_map/all_gather | solution.py:21
  7.9 143.0 %all-gather.5.cloned.1.call-start = ((), (), s32[]{:S(2)}) async-start(), calls=%async_computation.3 | async-start | bytes 2162688 | tf_op jit(solution)/shard_map/all_gather | solution.py:22
  8.6 230.4 %copy-start = (bf16[512]{0:T(512)(128)(2,1)S(1)}, bf16[512]{0:T(512)(128)(2,1)}, u32[]{:S(2)}) copy-start(bf16[512]{0:T(512)(128)(2,1)} %param.5) | copy-start | bytes 3076
  8.7 524.2 %reduce-scatter.7.cloned.1.call-start = ((), (), s32[]{:S(2)}) async-start(), calls=%async_computation.4 | async-start | bytes 2228224
  443.3 1.6 copy-start.1
  448.8 188.2 %reduce-scatter.9.cloned.1.call-start = ((), (), s32[]{:S(2)}) async-start(), calls=%async_computation.5 | async-start | bytes 2162688
Sparse Core Ops, SparseCore 0:
  10.0 83.7 all-gather.2
  96.9 53.9 all-gather.4
  448.9 83.9 reduce-scatter.6
  537.7 99.1 reduce-scatter.8
where the time goes:
time: 644 us; the launch traced here: 643 us
  waiting for transfers between devices  324 us (50%)
  blocking collectives  287 us (45%)
  between operations  13.8 us (2%)
  local copies, waits for them, and re-layouts  8.86 us (1%)
  matrix products  7.84 us (1%)
    unnamed x6, waiting for transfers between devices  181 us
    psum x3, blocking collectives, per_device(): column_mass = lax.psum(jnp.sum(transport, axis=0), 'sample')  171 us
    psum x3, blocking collectives, row_total(): return lax.psum(jnp.sum(values, axis=1), 'cls')  85.2 us
    all_gather x1, waiting for transfers between devices, per_device(): whole = lax.all_gather(features, 'cls', axis=1, tiled=True)  85 us
    all_gather x1, waiting for transfers between devices, per_device(): head_full = lax.all_gather(head, 'sample', axis=0, tiled=True)  57.1 us
    psum x1, blocking collectives, per_device(): lax.psum((jnp.sum(student, axis=1), jnp.sum(transport, axis=1)), 'cls')  31.3 us
  transfers between devices with their start and end apart: 4, of which 4 were waited for; matrix products, arithmetic and copies ran while one was open for 1% of the time, Pallas kernels for 0%

commit v1 on v0

--- a/solution.py
+++ b/solution.py
@@ -9,7 +9,7 @@
 
 
 def row_total(values):
-    return lax.psum(jnp.sum(values, axis=1), "cls")
+    return jnp.sum(lax.all_gather(jnp.sum(values, axis=1), "cls"), axis=0)
 
 
 def per_device(features, head, class_cap):

time: 644 us -> 669 us (1.039)
  blocking collectives: 287 us -> 312 us
    psum x3 -> x0, blocking collectives: 85.2 us -> none  [row_total(): return lax.psum(jnp.sum(values, axis=1), 'cls')]
    all_gather x0 -> x3, blocking collectives: none -> 82.1 us  [row_total(): return jnp.sum(lax.all_gather(jnp.sum(values, axis=1), 'cls'), axis=0)]
    psum x1 -> x2, blocking collectives: 31.3 us -> 59.7 us  [per_device(): lax.psum((jnp.sum(student, axis=1), jnp.sum(transport, axis=1)), 'cls')]
where the time goes in v1:
time: 669 us
  waiting for transfers between devices  323 us (48%)
  blocking collectives  312 us (47%)
  between operations  13.8 us (2%)
  local copies, waits for them, and re-layouts  8.86 us (1%)
  matrix products  7.85 us (1%)
    unnamed x6, waiting for transfers between devices  181 us
    psum x3, blocking collectives, per_device(): column_mass = lax.psum(jnp.sum(transport, axis=0), 'sample')  171 us
    all_gather x1, waiting for transfers between devices, per_device(): whole = lax.all_gather(features, 'cls', axis=1, tiled=True)  85 us
    all_gather x3, blocking collectives, row_total(): return jnp.sum(lax.all_gather(jnp.sum(values, axis=1), 'cls'), axis=0)  82.1 us
    psum x2, blocking collectives, per_device(): lax.psum((jnp.sum(student, axis=1), jnp.sum(transport, axis=1)), 'cls')  59.7 us
    all_gather x1, waiting for transfers between devices, per_device(): head_full = lax.all_gather(head, 'sample', axis=0, tiled=True)  57.1 us
  transfers between devices with their start and end apart: 4, of which 4 were waited for; matrix products, arithmetic and copies ran while one was open for 1% of the time, Pallas kernels for 0%

profile of v1, /device:TPU:2, one launch (start us, length us, event | category | flops | bytes accessed | tf_op | source)
XLA Modules:
  0.0 668.5 jit_solution(9500383681080833258)
XLA Ops:
  7.2 0.7 all-gather.9.cloned.1.call-update
  7.9 0.7 all-gather.11.cloned.1.call-update
  8.7 85.0 %all-gather.9.cloned.1.call-done = bf16[512,2048]{1,0:T(8,128)(2,1)} async-done(((bf16[512,128]{1,0:T(8,128)(2,1)}), bf16[512,2048]{1,0:T(8,128)(2,1)}) %all-gather.9.cloned.1.call-update) | async-done | bytes 2097168 | tf_op jit(solution)/shard_map/all_gather | solution.py:21
  93.7 57.1 %all-gather.11.cloned.1.call-done = bf16[2048,512]{1,0:T(8,128)(2,1)} async-done(((bf16[64,512]{1,0:T(8,128)(2,1)}), bf16[2048,512]{1,0:T(8,128)(2,1)}) %all-gather.11.cloned.1.call-update) | async-done | bytes 2097168 | tf_op jit(solution)/shard_map/all_gather | solution.py:22
  150.9 3.7 fusion.5
  154.6 31.3 %psum.35 = f32[512]{0:T(512)S(1)} all-reduce(f32[512]{0:T(512)S(1)} %get-tuple-element.15), channel_id=1, replica_groups=mesh['sample'=32,'cls'=16] {'cls'}, use_global_device_ids=true, to_apply=%region_1.0 | all-reduce | flops 512 | bytes 4096 | tf_op jit(solution)/shard_map/psum | solution.py:27
  186.1 53.0 %psum.36 = f32[512]{0:T(512)S(1)} all-reduce(f32[512]{0:T(512)S(1)} %fusion.12), channel_id=1, replica_groups=mesh['sample'=32,'cls'=16] {'sample'}, use_global_device_ids=true, to_apply=%region_3.0 | all-reduce | flops 512 | bytes 4096 | tf_op jit(solution)/shard_map/psum | solution.py:36
  239.1 0.4 fusion.3
  239.5 28.4 %psum.39 = f32[512]{0:T(512)S(1)} all-reduce(f32[512]{0:T(512)S(1)} %get-tuple-element.9), channel_id=1, replica_groups=mesh['sample'=32,'cls'=16] {'cls'}, use_global_device_ids=true, to_apply=%region_15.0 | all-reduce | flops 512 | bytes 4096 | tf_op jit(solution)/shard_map/psum | solution.py:27
  267.8 27.9 %all-gather.3 = f32[16,1,512]{2,1,0:T(1,128)S(1)} all-gather(f32[1,1,512]{2,1,0:T(1,128)S(1)} %bitcast.17), channel_id=2, replica_groups=mesh['sample'=32,'cls'=16] {'cls'}, dimensions={0}, use_global_device_ids=true | all-gather | bytes 34816 | tf_op jit(solution)/shard_map/all_gather | solution.py:12
  296.2 55.0 %psum.37 = f32[512]{0:T(512)S(1)} all-reduce(f32[512]{0:T(512)S(1)} %get-tuple-element.13), channel_id=1, replica_groups=mesh['sample'=32,'cls'=16] {'sample'}, use_global_device_ids=true, to_apply=%region_7.0 | all-reduce | flops 512 | bytes 4096 | tf_op jit(solution)/shard_map/psum | solution.py:36
  351.3 26.9 %all-gather.4 = f32[16,1,512]{2,1,0:T(1,128)S(1)} all-gather(f32[1,1,512]{2,1,0:T(1,128)S(1)} %bitcast.18), channel_id=3, replica_groups=mesh['sample'=32,'cls'=16] {'cls'}, dimensions={0}, use_global_device_ids=true | all-gather | bytes 34816 | tf_op jit(solution)/shard_map/all_gather | solution.py:12
  378.6 62.7 %psum.38 = f32[512]{0:T(512)S(1)} all-reduce(f32[512]{0:T(512)S(1)} %fusion.13), channel_id=1, replica_groups=mesh['sample'=32,'cls'=16] {'sample'}, use_global_device_ids=true, to_apply=%region_11.0 | all-reduce | flops 512 | bytes 4096 | tf_op jit(solution)/shard_map/psum | solution.py:36
  441.5 27.2 %all-gather.5 = f32[16,1,512]{2,1,0:T(1,128)S(1)} all-gather(f32[1,1,512]{2,1,0:T(1,128)S(1)} %bitcast.19), channel_id=4, replica_groups=mesh['sample'=32,'cls'=16] {'cls'}, dimensions={0}, use_global_device_ids=true | all-gather | bytes 34816 | tf_op jit(solution)/shard_map/all_gather | solution.py:12
  468.7 0.5 multiply_convert_fusion
  469.2 1.1 copy-done.1
  470.3 1.3 fusion
  471.7 2.6 copy.10
  474.3 2.8 fusion.1
  477.1 2.5 copy.12
  479.7 1.0 copy.8
  480.7 77.1 %reduce-scatter.7.cloned.1.call-done = bf16[128,512]{1,0:T(8,128)(2,1)} async-done(((bf16[2048,512]{1,0:T(8,128)(2,1)}), bf16[128,512]{1,0:T(8,128)(2,1)}) %reduce-scatter.7.cloned.1.call-update) | async-done | bytes 131088
  557.8 1.7 copy.11
  559.5 102.5 %reduce-scatter.9.cloned.1.call-done = bf16[64,512]{1,0:T(8,128)(2,1)} async-done(((bf16[2048,512]{1,0:T(8,128)(2,1)}), bf16[64,512]{1,0:T(8,128)(2,1)}) %reduce-scatter.9.cloned.1.call-update) | async-done | bytes 65552
  (20 shorter events, 1.6 us)
Async XLA Ops:
  7.2 86.6 %all-gather.9.cloned.1.call-start = ((), (), s32[]{:S(2)}) async-start(), calls=%async_computation.2 | async-start | bytes 2228224 | tf_op jit(solution)/shard_map/all_gather | solution.py:21
  7.9 143.0 %all-gather.11.cloned.1.call-start = ((), (), s32[]{:S(2)}) async-start(), calls=%async_computation.3 | async-start | bytes 2162688 | tf_op jit(solution)/shard_map/all_gather | solution.py:22
  8.6 230.4 %copy-start = (bf16[512]{0:T(512)(128)(2,1)S(1)}, bf16[512]{0:T(512)(128)(2,1)}, u32[]{:S(2)}) copy-start(bf16[512]{0:T(512)(128)(2,1)} %param.5) | copy-start | bytes 3076
  8.7 549.2 %reduce-scatter.7.cloned.1.call-start = ((), (), s32[]{:S(2)}) async-start(), calls=%async_computation.4 | async-start | bytes 2228224
  468.7 1.6 copy-start.1
  474.2 187.7 %reduce-scatter.9.cloned.1.call-start = ((), (), s32[]{:S(2)}) async-start(), calls=%async_computation.5 | async-start | bytes 2162688
Sparse Core Ops, SparseCore 0:
  10.0 83.7 all-gather.8
  96.9 53.9 all-gather.10
  474.4 83.4 reduce-scatter.6
  562.7 99.2 reduce-scatter.8
